TPU v7x, 32 devices: a whole 2x2x4 slice. The times are simulated.
32 devices in a mesh: row: 8 (over z, y), col: 4 (over x, core).
Axes of the slice: x: 2, y: 2, z: 4, core: 2. Of those that a mesh axis runs over, the one named last changes fastest.
Arguments:
- env: float32 [512, 32768], P('row', 'col'), may hold values from -0.03125 to 0.03125
- wave: float32 [32768, 512], P('row', 'col'), may hold values from -6 to 6
- mpo: float32 [16, 16], replicated, may hold values from -1.5 to 1.5
Outputs:
- applied: float32 [512, 512], P('row', 'col')
All inputs are finite; a program needn't handle non-finite values.
Results may differ from a plain program's by a relative error of at most 0.00007.
Values sent between devices are 32-bit elements; how exact they have to be, the bound alone decides.
No kernel may reach another device: no remote copies, remote signals or barrier semaphores. Data moves between devices by JAX's collectives and lax.ppermute only.
A program may use at most 128 MiB of HBM per device.

v0:
```python
import jax
import jax.numpy as jnp
from jax import lax
from jax.sharding import PartitionSpec as P


def shards(env, wave, mpo):
    spins = mpo.shape[0]
    env_full = lax.all_gather(env, "col", axis=1, tiled=True)
    right_local = wave.shape[1] // spins
    partial_out = jnp.dot(
        env_full,
        lax.all_gather(wave, "row", axis=0, tiled=True),
        precision=lax.Precision.HIGHEST,
        preferred_element_type=jnp.float32,
    )
    out3 = partial_out.reshape(env.shape[0], right_local, spins)
    mixed = jnp.einsum("irs,st->itr", out3, mpo, precision=lax.Precision.HIGHEST)
    spun = lax.all_to_all(mixed, "col", split_axis=1, concat_axis=2, tiled=True)
    return spun.reshape(env.shape[0], -1)


def solution(mesh):
    in_specs = (P("row", "col"), P("row", "col"), P())
    out_specs = P("row", "col")
    return jax.shard_map(shards, mesh=mesh, in_specs=in_specs, out_specs=out_specs, check_vma=False)
```

profile of v0, /device:TPU:0, one launch (start us, length us, event | category | flops | bytes accessed | tf_op | source)
XLA Modules:
  0.0 345.3 jit_solution(17700859789182060455)
XLA Ops:
  6.5 0.0 copy-start
  6.5 0.0 all-gather.3.cloned.1.call-start
  6.5 0.7 all-gather.3.cloned.1.call-update
  7.3 0.0 all-gather.5.cloned.1.call-start
  7.3 0.7 all-gather.5.cloned.1.call-update
  8.0 61.9 %all-gather.3.cloned.1.call-done = f32[64,32768]{1,0:T(8,128)} async-done(((f32[64,8192]{1,0:T(8,128)}), f32[64,32768]{1,0:T(8,128)}) %all-gather.3.cloned.1.call-update) | async-done | bytes 8388624 | tf_op jit(solution)/shard_map/all_gather | solution.py:9
  69.9 229.4 %all-gather.5.cloned.1.call-done = f32[32768,128]{1,0:T(8,128)} async-done(((f32[4096,128]{1,0:T(8,128)}), f32[32768,128]{1,0:T(8,128)}) %all-gather.5.cloned.1.call-update) | async-done | bytes 16777232 | tf_op jit(solution)/shard_map/all_gather | solution.py:13
  299.4 30.2 %fusion.1 = f32[64,128]{0,1:T(8,128)S(1)} fusion(f32[64,32768]{1,0:T(8,128)} %all-gather.3.cloned.1.call-done, f32[32768,128]{1,0:T(8,128)} %all-gather.5.cloned.1.call-done), kind=kOutput, calls=%fused_computation.3 | convolution fusion | flops 3221225472 | bytes 25198592 | tf_op jit(solution)/shard_map/dot_general | solution.py:11
  329.5 0.0 copy-done
  329.5 0.3 convolution_bitcast_fusion
  329.8 0.1 reshape.10
  329.9 6.5 %all_to_all.15 = f32[4,1,2048]{2,1,0:T(1,128)S(1)} all-to-all(f32[4,1,2048]{2,1,0:T(1,128)S(1)} %reshape.10), channel_id=1, replica_groups=mesh['row'=8,'col'=4] {'col'}, dimensions={0} | all-to-all | bytes 65536 | tf_op jit(solution)/shard_map/all_to_all | solution.py:19
  336.4 0.5 broadcast
  336.9 0.7 reduce
  337.7 0.1 reshape.11
  337.8 0.7 copy.15
  (2 shorter events, 0.0 us)
Async XLA Ops:
  6.5 323.0 %copy-start = (f32[16,16]{1,0:T(8,128)S(1)}, f32[16,16]{1,0:T(8,128)}, u32[]{:S(2)}) copy-start(f32[16,16]{1,0:T(8,128)} %param.5) | copy-start | bytes 3076
  6.5 63.4 %all-gather.3.cloned.1.call-start = ((), (), s32[]{:S(2)}) async-start(), calls=%async_computation.1 | async-start | bytes 10485760 | tf_op jit(solution)/shard_map/all_gather | solution.py:9
  7.3 292.1 %all-gather.5.cloned.1.call-start = ((), (), s32[]{:S(2)}) async-start(), calls=%async_computation.2 | async-start | bytes 18874368 | tf_op jit(solution)/shard_map/all_gather | solution.py:13
Sparse Core Ops, SparseCore 0:
  8.9 60.9 all-gather.2
  72.0 227.2 all-gather.4
where the time goes:
time: 345 us
  waiting for transfers between devices  293 us (85%)
  matrix products  30.4 us (9%)
  between operations  13.4 us (4%)
  blocking collectives  6.49 us (2%)
    all_gather x1, waiting for transfers between devices, shards(): lax.all_gather(wave, 'row', axis=0, tiled=True)  229 us
    all_gather x1, waiting for transfers between devices, shards(): env_full = lax.all_gather(env, 'col', axis=1, tiled=True)  61.9 us
    dot_general x1, matrix products, shards(): jnp.dot(env_full, lax.all_gather(wave, 'row', axis=0, tiled=True), precis...  30.2 us
  transfers between devices with their start and end apart: 2, of which 2 were waited for; matrix products, arithmetic and copies ran while one was open for 0% of the time, Pallas kernels for 0%

commit v1 on v0

--- a/solution.py
+++ b/solution.py
@@ -6,7 +6,8 @@
 
 def shards(env, wave, mpo):
     spins = mpo.shape[0]
-    env_full = lax.all_gather(env, "col", axis=1, tiled=True)
+    pieces = lax.all_gather(env, "col")
+    env_full = jnp.concatenate(pieces, axis=1)
     right_local = wave.shape[1] // spins
     partial_out = jnp.dot(
         env_full,

time: 345 us -> 333 us (0.965)
  waiting for transfers between devices: 293 us -> 266 us
  local copies, waits for them, and re-layouts: 1.44 us -> 28.4 us
  matrix products: 30.4 us -> 17.3 us
    all_gather x1, waiting for transfers between devices: 229 us -> 205 us  [shards(): lax.all_gather(wave, 'row', axis=0, tiled=True)]
    dot_general x1, matrix products: 30.2 us -> 17 us  [shards(): jnp.dot(env_full, lax.all_gather(wave, 'row', axis=0, tiled=True), precis...]
    all_gather x0 -> x1, local copies, waits for them, and re-layouts: none -> 12.9 us  [shards(): pieces = lax.all_gather(env, 'col')]
    reshape x0 -> x1, local copies, waits for them, and re-layouts: none -> 11.1 us  [shards(): env_full = jnp.concatenate(pieces, axis=1)]
  transfers between devices with their start and end apart: 2 -> 2, of which waited for: 2 -> 2; matrix products, arithmetic and copies ran while one was open for 0% -> 8% of each run, Pallas kernels for 0% -> 0%
where the time goes in v1:
time: 333 us; the launch traced here: 332 us
  waiting for transfers between devices  266 us (80%)
  local copies, waits for them, and re-layouts  28.4 us (9%)
  matrix products  17.3 us (5%)
  between operations  13.4 us (4%)
  blocking collectives  6.48 us (2%)
    all_gather x1, waiting for transfers between devices, shards(): lax.all_gather(wave, 'row', axis=0, tiled=True)  205 us
    all_gather x1, waiting for transfers between devices, shards(): pieces = lax.all_gather(env, 'col')  59.6 us
    dot_general x1, matrix products, shards(): jnp.dot(env_full, lax.all_gather(wave, 'row', axis=0, tiled=True), precis...  17 us
    all_gather x1, local copies, waits for them, and re-layouts, shards(): pieces = lax.all_gather(env, 'col')  12.9 us
    reshape x1, local copies, waits for them, and re-layouts, shards(): env_full = jnp.concatenate(pieces, axis=1)  11.1 us
  transfers between devices with their start and end apart: 2, of which 2 were waited for; matrix products, arithmetic and copies ran while one was open for 8% of the time, Pallas kernels for 0%

profile of v1, /device:TPU:0, one launch (start us, length us, event | category | flops | bytes accessed | tf_op | source)
XLA Modules:
  0.0 332.2 jit_solution(18391022044281780472)
XLA Ops:
  6.5 0.0 copy-start
  6.5 0.0 all-gather.6.cloned.1.call-start
  6.5 0.7 all-gather.6.cloned.1.call-update
  7.3 0.0 all-gather.4.cloned.1.call-start
  7.3 2.9 copy.12
  10.2 0.0 all-gather.4.cloned.1.call-update
  10.3 59.6 %all-gather.6.cloned.1.call-done = f32[256,8192]{1,0:T(8,128)} async-done(((f32[64,8192]{1,0:T(8,128)}), f32[256,8192]{1,0:T(8,128)}) %all-gather.6.cloned.1.call-update) | async-done | bytes 8388624 | tf_op jit(solution)/shard_map/all_gather | solution.py:9
  69.9 12.9 %copy.21 = f32[4,64,8192]{2,0,1:T(4,128)} copy(f32[4,64,8192]{2,1,0:T(8,128)} %bitcast.25) | data formatting | bytes 16777216 | tf_op jit(solution)/shard_map/all_gather | solution.py:9
  82.8 11.1 %reshape.16 = f32[64,32768,1]{1,0,2:T(8,128)} reshape(f32[64,4,8192]{2,1,0:T(4,128)} %bitcast.23) | data formatting | bytes 16777216 | tf_op jit(solution)/shard_map/reshape | solution.py:10
  93.9 205.5 %all-gather.4.cloned.1.call-done = f32[32768,128]{0,1:T(8,128)} async-done(((f32[4096,128]{0,1:T(8,128)}), f32[32768,128]{0,1:T(8,128)}) %all-gather.4.cloned.1.call-update) | async-done | bytes 16777232 | tf_op jit(solution)/shard_map/all_gather | solution.py:14
  299.4 17.0 %fusion.1 = f32[64,8,16]{0,2,1:T(8,128)S(1)} fusion(f32[64,32768,1]{1,0,2:T(8,128)} %reshape.16, f32[8,16,32768]{2,1,0:T(8,128)} %bitcast.24), kind=kOutput, calls=%fused_computation.4 | convolution fusion | flops 3221225472 | bytes 25198592 | tf_op jit(solution)/shard_map/dot_general | solution.py:12
  316.4 0.0 copy-done
  316.4 0.3 convolution_bitcast_fusion
  316.7 0.1 reshape.19
  316.8 6.5 %all_to_all.15 = f32[4,1,2048]{2,1,0:T(1,128)S(1)} all-to-all(f32[4,1,2048]{2,1,0:T(1,128)S(1)} %reshape.19), channel_id=1, replica_groups=mesh['row'=8,'col'=4] {'col'}, dimensions={0} | all-to-all | bytes 65536 | tf_op jit(solution)/shard_map/all_to_all | solution.py:20
  323.3 0.5 broadcast
  323.8 0.7 reduce
  324.6 0.1 reshape.20
  324.7 0.7 copy.16
  (2 shorter events, 0.0 us)
Async XLA Ops:
  6.5 309.9 %copy-start = (f32[16,16]{1,0:T(8,128)S(1)}, f32[16,16]{1,0:T(8,128)}, u32[]{:S(2)}) copy-start(f32[16,16]{1,0:T(8,128)} %param.5) | copy-start | bytes 3076
  6.5 63.4 %all-gather.6.cloned.1.call-start = ((), (), s32[]{:S(2)}) async-start(), calls=%async_computation.2 | async-start | bytes 10485760 | tf_op jit(solution)/shard_map/all_gather | solution.py:9
  7.3 292.1 %all-gather.4.cloned.1.call-start = ((), (), s32[]{:S(2)}) async-start(), calls=%async_computation.1 | async-start | bytes 18874368 | tf_op jit(solution)/shard_map/all_gather | solution.py:14
Sparse Core Ops, SparseCore 0:
  8.9 60.9 all-gather.5
  72.1 227.2 all-gather.3

commit v2 on v0

--- a/solution.py
+++ b/solution.py
@@ -1,7 +1,23 @@
+import functools
 import jax
 import jax.numpy as jnp
 from jax import lax
 from jax.sharding import PartitionSpec as P
+
+
+def hold_the_quotas(x_part, link_axis, row_dim):
+    return jnp.concatenate(
+        jax.lax.all_to_all(
+            jnp.stack([x_part for _ in range(jax.lax.axis_size(link_axis))]),
+            axis_name=link_axis,
+            split_axis=0,
+            concat_axis=0,
+        ),
+        row_dim,
+    )
+
+
+handle_shifts_all = functools.partial(hold_the_quotas, link_axis="row", row_dim=0)
 
 
 def shards(env, wave, mpo):
@@ -10,7 +26,7 @@
     right_local = wave.shape[1] // spins
     partial_out = jnp.dot(
         env_full,
-        lax.all_gather(wave, "row", axis=0, tiled=True),
+        handle_shifts_all(wave),
         precision=lax.Precision.HIGHEST,
         preferred_element_type=jnp.float32,
     )

time: 345 us -> 431 us (1.25)
  waiting for transfers between devices: 293 us -> 363 us
  local copies, waits for them, and re-layouts: 1.44 us -> 22.9 us
  matrix products: 30.4 us -> 17.3 us
  starting transfers between devices: 0.04 us -> 7.35 us
    all_to_all x0 -> x1, waiting for transfers between devices: none -> 362 us  [hold_the_quotas(): jax.lax.all_to_all(jnp.stack([x_part for _ in range(jax.lax.axis_size(lin...]
    all_gather x1 -> x0, waiting for transfers between devices: 229 us -> none  [shards(): lax.all_gather(wave, 'row', axis=0, tiled=True)]
    all_gather x1, waiting for transfers between devices: 61.9 us -> 0.01 us  [shards(): env_full = lax.all_gather(env, 'col', axis=1, tiled=True)]
    dot_general x1, matrix products: 30.2 us -> 17 us  [shards(): jnp.dot(env_full, handle_shifts_all(wave), precision=lax.Precision.HIGHES...]
    reshape x0 -> x1, local copies, waits for them, and re-layouts: none -> 11.6 us  [hold_the_quotas(): jnp.concatenate(jax.lax.all_to_all(jnp.stack([x_part for _ in range(jax.l...]
    another operation x0 -> x1, local copies, waits for them, and re-layouts: none -> 8.01 us  [hold_the_quotas(): jnp.stack([x_part for _ in range(jax.lax.axis_size(link_axis))])]
    all_to_all x0 -> x1, starting transfers between devices: none -> 7.31 us  [hold_the_quotas(): jax.lax.all_to_all(jnp.stack([x_part for _ in range(jax.lax.axis_size(lin...]
  transfers between devices with their start and end apart: 2 -> 2, of which waited for: 2 -> 1; matrix products, arithmetic and copies ran while one was open for 0% -> 3% of each run, Pallas kernels for 0% -> 0%
where the time goes in v2:
time: 431 us
  waiting for transfers between devices  363 us (84%)
  local copies, waits for them, and re-layouts  22.9 us (5%)
  matrix products  17.3 us (4%)
  between operations  13.4 us (3%)
  starting transfers between devices  7.35 us (2%)
  blocking collectives  6.53 us (2%)
    all_to_all x1, waiting for transfers between devices, hold_the_quotas(): jax.lax.all_to_all(jnp.stack([x_part for _ in range(jax.lax.axis_size(lin...  362 us
    dot_general x1, matrix products, shards(): jnp.dot(env_full, handle_shifts_all(wave), precision=lax.Precision.HIGHES...  17 us
    reshape x1, local copies, waits for them, and re-layouts, hold_the_quotas(): jnp.concatenate(jax.lax.all_to_all(jnp.stack([x_part for _ in range(jax.l...  11.6 us
  transfers between devices with their start and end apart: 2, of which 1 were waited for; matrix products, arithmetic and copies ran while one was open for 3% of the time, Pallas kernels for 0%

profile of v2, /device:TPU:0, one launch (start us, length us, event | category | flops | bytes accessed | tf_op | source)
XLA Modules:
  0.0 431.2 jit_solution(17038310583289702271)
XLA Ops:
  6.5 0.0 copy-start
  6.5 1.9 copy.10
  8.5 8.0 %stack.2 = f32[8,4096,128]{1,2,0:T(8,128)} broadcast(f32[4096,128]{0,1:T(8,128)S(1)} %copy.10), dimensions={1,2} | broadcast | bytes 18874368 | tf_op jit(solution)/shard_map/stack | solution.py:11
  16.5 7.3 %all-to-all-start = ((f32[8,4096,128]{1,2,0:T(8,128)}), f32[8,4096,128]{1,2,0:T(8,128)}, u32[]{:S(2)}, u32[]{:S(2)}) async-start(f32[8,4096,128]{1,2,0:T(8,128)} %stack.2), calls=%async_computation | async-start | bytes 33554432 | tf_op jit(solution)/shard_map/all_to_all | solution.py:10
  23.8 0.0 all-gather.2.cloned.1.call-start
  23.8 0.7 all-gather.2.cloned.1.call-update
  24.5 362.3 %all-to-all-done = f32[8,4096,128]{1,2,0:T(8,128)} async-done(((f32[8,4096,128]{1,2,0:T(8,128)}), f32[8,4096,128]{1,2,0:T(8,128)}, u32[]{:S(2)}, u32[]{:S(2)}) %all-to-all-start) | async-done | bytes 16777248 | tf_op jit(solution)/shard_map/all_to_all | solution.py:10
  386.8 11.6 %copy.18 = f32[8,16,8,4096]{3,2,0,1:T(8,128)} copy(f32[8,16,8,4096]{3,2,1,0:T(8,128)} %bitcast.10) | data formatting | bytes 33554432 | tf_op jit(solution)/shard_map/reshape | solution.py:9
  398.4 0.0 all-gather.2.cloned.1.call-done
  398.4 17.0 %fusion = f32[64,8,16]{0,2,1:T(8,128)S(1)} fusion(f32[8,16,32768]{2,1,0:T(8,128)} %bitcast.24, f32[64,32768]{1,0:T(8,128)} %all-gather.2.cloned.1.call-done), kind=kOutput, calls=%fused_computation | convolution fusion | flops 3221225472 | bytes 25198592 | tf_op jit(solution)/shard_map/dot_general | solution.py:27
  415.4 0.0 copy-done
  415.4 0.3 convolution_bitcast_fusion
  415.7 0.1 reshape.15
  415.8 6.5 %all_to_all.20 = f32[4,1,2048]{2,1,0:T(1,128)S(1)} all-to-all(f32[4,1,2048]{2,1,0:T(1,128)S(1)} %reshape.15), channel_id=1, replica_groups=mesh['row'=8,'col'=4] {'col'}, dimensions={0} | all-to-all | bytes 65536 | tf_op jit(solution)/shard_map/all_to_all | solution.py:35
  422.3 0.5 broadcast.2
  422.8 0.7 reduce
  423.6 0.1 reshape.16
  423.7 0.7 copy.15
  (2 shorter events, 0.0 us)
Async XLA Ops:
  6.5 408.9 %copy-start = (f32[16,16]{1,0:T(8,128)S(1)}, f32[16,16]{1,0:T(8,128)}, u32[]{:S(2)}) copy-start(f32[16,16]{1,0:T(8,128)} %param.5) | copy-start | bytes 3076
  16.5 370.3 %all-to-all-start = ((f32[8,4096,128]{1,2,0:T(8,128)}), f32[8,4096,128]{1,2,0:T(8,128)}, u32[]{:S(2)}, u32[]{:S(2)}) async-start(f32[8,4096,128]{1,2,0:T(8,128)} %stack.2), calls=%async_computation | async-start | bytes 33554432 | tf_op jit(solution)/shard_map/all_to_all | solution.py:10
  23.8 374.6 %all-gather.2.cloned.1.call-start = ((), (), s32[]{:S(2)}) async-start(), calls=%async_computation.2 | async-start | bytes 10485760 | tf_op jit(solution)/shard_map/all_gather | solution.py:25
Sparse Core Ops, SparseCore 0:
  26.2 59.6 all-gather.1
